TPU v7x, 32 devices: a whole 2x2x4 slice. The times are simulated.
32 devices in a mesh: row: 8 (over y, x, core), col: 4 (over z).
Axes of the slice: x: 2, y: 2, z: 4, core: 2. Of those that a mesh axis runs over, the one named last changes fastest.
Arguments:
- in_map: bfloat16 [128, 128, 256], P('row', 'col'), may hold values from -6 to 6
- tile_w: bfloat16 [3, 3, 256, 256], replicated, may hold values from -0.125 to 0.125
- head_w1: bfloat16 [3, 3, 256, 256], replicated, may hold values from -0.125 to 0.125
- head_w2: bfloat16 [3, 3, 256, 256], replicated, may hold values from -0.125 to 0.125
- box_row: int32 [64, 4], P('row', 'col'), may hold values from 0 to 2
- box_col: int32 [64, 4], P('row', 'col'), may hold values from 0 to 18
- box_target: int32 [64, 4], P('row', 'col'), may hold values from -1 to 15, as said below
- head_cot: bfloat16 [32, 4, 14, 14, 256], P('row', 'col'), may hold values from -6 to 6
Outputs:
- grad_map: bfloat16 [128, 128, 256], P('row', 'col')
- grad_w1: float32 [3, 3, 256, 256], replicated
- grad_w2: float32 [3, 3, 256, 256], replicated
Inputs may be any that keep to these rules, and one draw needn't show every extreme that they name: `box_target`: within each row r of tiles, every head slot d * 4 + h (d below 4, h below 4) is named by exactly one tile slot, and empty slots hold -1. A tile names at most 2 head slots of one device, so it holds at most 8 boxes; in every row of tiles one tile holds 8 boxes, 2 for each device of the row.
All inputs are finite; a program needn't handle non-finite values.
Results may differ from a plain program's by a relative error of at most 0.012.
Values may be sent and summed in bfloat16 or wider, within the bound.
No kernel may reach another device: no remote copies, remote signals or barrier semaphores. Data moves between devices by JAX's collectives and lax.ppermute only.
A program may use at most 64 MiB of HBM per device.

v0:
```python
import math
import jax
import jax.numpy as jnp
from jax import lax
from jax.sharding import PartitionSpec as P

LAYOUT = ("NHWC", "HWIO", "NHWC")


def padded_2(shard, sides, width):
    for axis, dim in sides:
        size, length = (lax.axis_size(axis), shard.shape[dim])
        up = [(i, (i + 1) % size) for i in range(size - 1)]
        down = [(j, i) for i, j in up]
        last = lax.slice_in_dim(shard, length - width, length, axis=dim)
        leading = lax.slice_in_dim(shard, 0, width, axis=dim)
        before = lax.ppermute(last, axis, up)
        after = lax.ppermute(leading, axis, down)
        shard = jnp.concatenate([before, shard, after], axis=dim)
    return shard


def conv_pad(inputs, kernel, margin):
    return lax.conv_general_dilated(
        inputs,
        kernel,
        (1, 1),
        ((margin, margin), (margin, margin)),
        dimension_numbers=LAYOUT,
        preferred_element_type=jnp.float32,
    )


def flip_weights(kernel):
    return jnp.transpose(jnp.flip(kernel, (0, 1)), (0, 1, 3, 2))


def silu_slope(values):
    sigma = jax.nn.sigmoid(values)
    return sigma * (1.0 + values * (1.0 - sigma))


def weight_grad(inputs, deltas):
    channels = inputs.shape[-1]
    box_side = inputs.shape[1]
    padded = jnp.pad(inputs, ((0, 0), (1, 1), (1, 1), (0, 0)))
    flat_delta = deltas.reshape(-1, channels)
    blocks = []
    for shift_y in range(3):
        for shift_x in range(3):
            window = padded[
                :, shift_y : shift_y + box_side, shift_x : shift_x + box_side, :
            ].reshape(-1, channels)
            blocks.append(
                lax.dot_general(
                    window, flat_delta, (((0,), (0,)), ((), ())), preferred_element_type=jnp.float32
                )
            )
    return jnp.stack(blocks).reshape(3, 3, channels, channels)


def pick_rows(table, values):
    flat = values.reshape(values.shape[0], -1)
    return jnp.dot(table, flat, preferred_element_type=jnp.float32).astype(jnp.bfloat16)


def pick_back(table, values):
    return lax.dot_general(
        table, values, (((0,), (0,)), ((), ())), preferred_element_type=jnp.float32
    ).astype(jnp.bfloat16)


def body(in_map, tile_w, head_w1, head_w2, box_row, box_col, box_target, head_cot):
    tile_rows, tile_cols, channels = in_map.shape
    head_count = head_cot.shape[0]
    box_side = head_cot.shape[2]
    slot_count = box_target.shape[0]
    columns = lax.axis_size("col")
    capacity = slot_count // columns
    pair_count = columns * capacity
    padded = padded_2(in_map, (("row", 0), ("col", 1)), 1)
    preact = conv_pad(padded[None], tile_w, 0)[0]
    target = box_target[:, 0]
    occupied = target >= 0
    dest_col = jnp.where(occupied, target // head_count, 0)
    head_slot = jnp.where(occupied, target % head_count, 0)
    slot_ids = jnp.arange(slot_count, dtype=jnp.int32)
    same_dest = (dest_col[:, None] == dest_col[None, :]) & occupied[None, :]
    placing = jnp.sum(same_dest & (slot_ids[None, :] < slot_ids[:, None]), axis=1)
    pair_slot = dest_col * capacity + placing
    pair_ids = jnp.arange(pair_count, dtype=jnp.int32)
    send_map = ((pair_slot[None, :] == pair_ids[:, None]) & occupied[None, :]).astype(jnp.bfloat16)
    head_ids = jnp.arange(head_count, dtype=jnp.int32)
    head_hot = ((head_slot[:, None] == head_ids[None, :]) & occupied[:, None]).astype(jnp.bfloat16)
    pair_head = (
        jnp.dot(send_map, head_hot, preferred_element_type=jnp.float32)
        .astype(jnp.bfloat16)
        .reshape(columns, capacity, head_count)
    )
    top_row = box_row[:, 0]
    left_col = box_col[:, 0]
    zero_index = jnp.zeros((), jnp.int32)
    window = box_side + 2
    windows = jax.vmap(
        lambda y, x: lax.dynamic_slice(padded, (y, x, zero_index), (window, window, channels))
    )(top_row, left_col)
    outgoing = pick_rows(send_map, windows).reshape(columns, capacity, window, window, channels)
    arrived, arrived_head = (
        lax.all_to_all(outgoing, "col", split_axis=0, concat_axis=0, tiled=True),
        lax.all_to_all(pair_head, "col", split_axis=0, concat_axis=0, tiled=True),
    )
    arrived_head = arrived_head.reshape(pair_count, head_count)
    gathered = pick_back(arrived_head, arrived.reshape(pair_count, -1)).reshape(
        head_count, window, window, channels
    )
    box_input = jax.nn.silu(conv_pad(gathered, tile_w, 0)).astype(jnp.bfloat16)
    factor = 1.0 / math.sqrt(lax.axis_size("row") * columns * head_count * box_side * box_side)
    cotangent = head_cot[:, 0]
    pre_one = conv_pad(box_input, head_w1, 1)
    hidden = jax.nn.silu(pre_one).astype(jnp.bfloat16)
    pre_two = conv_pad(hidden, head_w2, 1)
    delta_two = (cotangent.astype(jnp.float32) * silu_slope(pre_two)).astype(jnp.bfloat16)
    second_local = weight_grad(hidden, delta_two)
    delta_one = (conv_pad(delta_two, flip_weights(head_w2), 1) * silu_slope(pre_one)).astype(
        jnp.bfloat16
    )
    box_grads = conv_pad(delta_one, flip_weights(head_w1), 1).astype(jnp.bfloat16)
    sent_back = pick_rows(arrived_head, box_grads).reshape(
        columns, capacity, box_side, box_side, channels
    )
    returned = lax.all_to_all(sent_back, "col", split_axis=0, concat_axis=0, tiled=True)
    slot_grads = pick_back(send_map, returned.reshape(pair_count, -1)).reshape(
        slot_count, box_side, box_side, channels
    )
    first_local = weight_grad(box_input, delta_one)
    first_sum, second_sum = lax.psum((first_local, second_local), ("row", "col"))

    def add_box(slot, running):
        current = lax.dynamic_slice(
            running, (top_row[slot], left_col[slot], zero_index), (box_side, box_side, channels)
        )
        return lax.dynamic_update_slice(
            running,
            current + slot_grads[slot].astype(jnp.float32),
            (top_row[slot], left_col[slot], zero_index),
        )

    box_total = lax.fori_loop(
        0, slot_count, add_box, jnp.zeros((tile_rows, tile_cols, channels), jnp.float32)
    )
    delta_map = (box_total * silu_slope(preact)).astype(jnp.bfloat16)
    delta_rim = padded_2(delta_map, (("row", 0), ("col", 1)), 1)
    grad_map = conv_pad(delta_rim[None], flip_weights(tile_w), 0)[0].astype(jnp.bfloat16)
    return (grad_map, first_sum * factor, second_sum * factor)


def solution(mesh):
    in_specs = (
        P("row", "col", None),
        P(),
        P(),
        P(),
        P("row", "col"),
        P("row", "col"),
        P("row", "col"),
        P("row", "col", None, None, None),
    )
    out_specs = (P("row", "col", None), P(), P())
    return jax.shard_map(body, mesh=mesh, in_specs=in_specs, out_specs=out_specs, check_vma=False)
```

profile of v0, /device:TPU:0, one launch (start us, length us, event | category | flops | bytes accessed | tf_op | source)
XLA Modules:
  0.0 296.8 jit_solution(2329614647910186350)
XLA Ops:
  8.0 1.3 collective-permute-start.1
  9.3 3.0 %collective-permute-start = (bf16[1,32,256]{2,1,0:T(8,128)(2,1)S(1)}, bf16[1,32,256]{2,1,0:T(8,128)(2,1)S(1)}, u32[]{:S(2)}, u32[]{:S(2)}) collective-permute-start(bf16[1,32,256]{2,1,0:T(8,128)(2,1)S(1)} %get-tuple-element.174), channel_id=1, source_target_pairs={{0,4},{4,8},{8,12},{12,16},{16,20},{20,24},{24,28},{1,5},{5,9},{9,... | collective-permute-start | bytes 49160 | tf_op jit(solution)/shard_map/ppermute | solution.py:17
  16.9 5.0 %collective-permute-start.2 = (bf16[18,1,256]{2,1,0:T(2,128)(2,1)S(1)}, bf16[18,1,256]{2,1,0:T(2,128)(2,1)S(1)}, u32[]{:S(2)}, u32[]{:S(2)}) collective-permute-start(bf16[18,1,256]{2,1,0:T(2,128)(2,1)S(1)} %get-tuple-element.169), channel_id=1, source_target_pairs={{0,1},{1,2},{2,3},{4,5},{5,6},{6,7},{8,9},{9,10},{10,11},{12,13},{... | collective-permute-start | bytes 27656 | tf_op jit(solution)/shard_map/ppermute | solution.py:17
  21.9 1.3 collective-permute-start.3
  23.3 4.3 %collective-permute-done.3 = bf16[18,1,256]{2,1,0:T(2,128)(2,1)S(1)} collective-permute-done((bf16[18,1,256]{2,1,0:T(2,128)(2,1)S(1)}, bf16[18,1,256]{2,1,0:T(2,128)(2,1)S(1)}, u32[]{:S(2)}, u32[]{:S(2)}) %collective-permute-start.3) | collective-permute-done | bytes 9248 | tf_op jit(solution)/shard_map/ppermute | solution.py:18
  27.8 20.0 %while.15 = (s32[]{:T(128)}, bf16[18,34,256]{2,1,0:T(8,128)(2,1)S(1)}, s32[8,3]{0,1:T(4,128)S(1)}, bf16[8,16,16,256]{3,2,1,0:T(8,128)(2,1)}, s32[]{:T(128)}) while((s32[]{:T(128)}, bf16[18,34,256]{2,1,0:T(8,128)(2,1)S(1)}, s32[8,3]{0,1:T(4,128)S(1)}, bf16[8,16,16,256]{3,2,1,0:T(8,128)(2,1)}, s32[]{:T(128)}) %tuple.64), condition=%wide.while_cond, body=%wide.while_body.sunk | while | flops 2 | bytes 263285 | solution.py:105
  28.4 1.9 bitcast_dynamic-update-slice_fusion.2
  30.9 1.9 bitcast_dynamic-update-slice_fusion.2
  33.4 1.9 bitcast_dynamic-update-slice_fusion.2
  35.9 1.9 bitcast_dynamic-update-slice_fusion.2
  38.4 1.9 bitcast_dynamic-update-slice_fusion.2
  40.9 1.9 bitcast_dynamic-update-slice_fusion.2
  43.4 1.9 bitcast_dynamic-update-slice_fusion.2
  45.9 1.9 bitcast_dynamic-update-slice_fusion.2
  47.8 1.8 copy.157
  50.0 1.2 copy.158
  51.2 4.0 %all-to-all-start.1 = ((bf16[4,2,16,16,256]{4,3,2,1,0:T(8,128)(2,1)}), bf16[4,2,16,16,256]{4,3,2,1,0:T(8,128)(2,1)S(1)}, u32[]{:S(2)}, u32[]{:S(2)}) async-start(bf16[4,2,16,16,256]{4,3,2,1,0:T(8,128)(2,1)} %bitcast.140), calls=%async_computation.1 | async-start | bytes 2097152 | tf_op jit(solution)/shard_map/all_to_all | solution.py:109
  57.3 1.1 copy.111
  58.4 22.7 %all-to-all-done.1 = bf16[4,2,16,16,256]{4,3,2,1,0:T(8,128)(2,1)S(1)} async-done(((bf16[4,2,16,16,256]{4,3,2,1,0:T(8,128)(2,1)}), bf16[4,2,16,16,256]{4,3,2,1,0:T(8,128)(2,1)S(1)}, u32[]{:S(2)}, u32[]{:S(2)}) %all-to-all-start.1) | async-done | bytes 1048608 | tf_op jit(solution)/shard_map/all_to_all | solution.py:109
  81.0 3.4 %all-to-all-start = ((bf16[4,2,4]{2,1,0:T(2,128)(2,1)}), bf16[4,2,4]{2,1,0:T(2,128)(2,1)S(1)}, u32[]{:S(2)}, u32[]{:S(2)}) async-start(bf16[4,2,4]{2,1,0:T(2,128)(2,1)} %bitcast.9), calls=%async_computation | async-start | bytes 4096 | tf_op jit(solution)/shard_map/all_to_all | solution.py:110
  84.9 4.8 %all-to-all-done = bf16[4,2,4]{2,1,0:T(2,128)(2,1)S(1)} async-done(((bf16[4,2,4]{2,1,0:T(2,128)(2,1)}), bf16[4,2,4]{2,1,0:T(2,128)(2,1)S(1)}, u32[]{:S(2)}, u32[]{:S(2)}) %all-to-all-start) | async-done | bytes 96 | tf_op jit(solution)/shard_map/all_to_all | solution.py:110
  90.9 1.3 multiply_convert_fusion.1
  93.4 1.2 fusion.43
  94.7 1.1 select_bitcast_fusion.1
  96.4 1.3 add_multiply_fusion
  99.1 1.2 fusion.62
  101.6 2.9 fusion.9
  106.2 2.3 copy.120
  108.4 1.2 reshape.164
  111.4 2.5 convolution_convert_fusion.4
  116.3 1.8 copy.105
  118.1 3.5 %all-to-all-start.2 = ((bf16[4,2,14,14,256]{4,1,3,2,0:T(2,128)(2,1)}), bf16[4,2,14,14,256]{4,1,3,2,0:T(2,128)(2,1)S(1)}, u32[]{:S(2)}, u32[]{:S(2)}) async-start(bf16[4,2,14,14,256]{4,1,3,2,0:T(2,128)(2,1)} %copy.105), calls=%async_computation.2 | async-start | bytes 1605632 | tf_op jit(solution)/shard_map/all_to_all | solution.py:131
  121.6 1.4 fusion.28
  130.5 1.1 fusion.17
  134.0 1.3 fusion.14
  136.5 1.1 fusion.12
  137.6 1.1 fusion.11
  138.6 1.8 all-to-all-done.2
  141.9 45.4 %while.14 = (s32[]{:T(128)}, f32[16,32,256]{2,0,1:T(8,128)S(1)}, s32[8]{0:T(128)S(1)}, s32[8]{0:T(128)S(1)}, bf16[8,14,14,256]{3,2,1,0:T(8,128)(2,1)S(1)}, /*index=5*/s32[]{:T(128)}, s32[]{:T(128)}, s32[]{:T(128)}, s32[]{:T(128)}) while((s32[]{:T(128)}, f32[16,32,256]{2,0,1:T(8,128)S(1)}, s32[8]{0:T(128)S(1)}, s32[8]{0:T(128)S(1)}, ...), condition=%wide.region_2.3_spmd, body=%wide.region_1.2_spmd.sunk | while | flops 100360 | bytes 1706193 | solution.py:148
  187.6 1.3 collective-permute-start.4
  188.9 1.3 collective-permute-start.5
  190.2 4.3 %collective-permute-done.5 = bf16[1,32,256]{2,0,1:T(2,128)(2,1)S(1)} collective-permute-done((bf16[1,32,256]{2,0,1:T(2,128)(2,1)S(1)}, bf16[1,32,256]{2,0,1:T(2,128)(2,1)S(1)}, u32[]{:S(2)}, u32[]{:S(2)}) %collective-permute-start.5) | collective-permute-done | bytes 16416 | tf_op jit(solution)/shard_map/ppermute | solution.py:18
  194.6 1.8 collective-permute-start.6
  196.4 1.3 collective-permute-start.7
  197.8 4.2 %collective-permute-done.7 = bf16[18,1,256]{2,0,1:T(8,128)(2,1)S(1)} collective-permute-done((bf16[18,1,256]{2,0,1:T(8,128)(2,1)S(1)}, bf16[18,1,256]{2,0,1:T(8,128)(2,1)S(1)}, u32[]{:S(2)}, u32[]{:S(2)}) %collective-permute-start.7) | collective-permute-done | bytes 9248 | tf_op jit(solution)/shard_map/ppermute | solution.py:18
  204.3 80.6 %all-reduce.5.cloned.1.call-done = (f32[3,3,256,256]{3,2,1,0:T(8,128)}, f32[3,3,256,256]{3,2,1,0:T(8,128)}) async-done(((f32[3,3,256,256]{3,2,1,0:T(8,128)}, f32[3,3,256,256]{3,2,1,0:T(8,128)}), (f32[3,3,256,256]{3,2,1,0:T(8,128)}, f32[3,3,256,256]{3,2,1,0:T(8,128)})) %all-reduce.5.cloned.1.call-update) | async-done | bytes 4718608 | tf_op jit(solution)/shard_map/psum | solution.py:136
  284.9 3.4 %broadcast_multiply_fusion.1 = f32[3,3,256,256]{3,2,1,0:T(8,128)} fusion(f32[3,3,256,256]{3,2,1,0:T(8,128)} %get-tuple-element.153), kind=kLoop, calls=%fused_computation.29 | loop fusion | flops 589824 | bytes 4718592 | tf_op jit(solution)/shard_map/mul | solution.py:154
  288.3 1.6 broadcast_multiply_fusion
  (196 shorter events, 53.8 us)
Async XLA Ops:
  7.2 49.2 %copy-start = (bf16[3,3,256,256]{3,2,1,0:T(8,128)(2,1)S(1)}, bf16[3,3,256,256]{3,2,1,0:T(8,128)(2,1)}, u32[]{:S(2)}) copy-start(bf16[3,3,256,256]{3,2,1,0:T(8,128)(2,1)} %param.11) | copy-start | bytes 3538948
  8.0 8.8 %collective-permute-start.1 = (bf16[1,32,256]{2,1,0:T(8,128)(2,1)S(1)}, bf16[1,32,256]{2,1,0:T(8,128)(2,1)S(1)}, u32[]{:S(2)}, u32[]{:S(2)}) collective-permute-start(bf16[1,32,256]{2,1,0:T(8,128)(2,1)S(1)} %get-tuple-element.173), channel_id=1, source_target_pairs={{4,0},{8,4},{12,8},{16,12},{20,16},{24,20},{28,24},{5,1},{9,5},{13... | collective-permute-start | bytes 49160 | tf_op jit(solution)/shard_map/ppermute | solution.py:18
  9.3 6.6 %collective-permute-start = (bf16[1,32,256]{2,1,0:T(8,128)(2,1)S(1)}, bf16[1,32,256]{2,1,0:T(8,128)(2,1)S(1)}, u32[]{:S(2)}, u32[]{:S(2)}) collective-permute-start(bf16[1,32,256]{2,1,0:T(8,128)(2,1)S(1)} %get-tuple-element.174), channel_id=1, source_target_pairs={{0,4},{4,8},{8,12},{12,16},{16,20},{20,24},{24,28},{1,5},{5,9},{9,... | collective-permute-start | bytes 49160 | tf_op jit(solution)/shard_map/ppermute | solution.py:17
  16.9 6.4 %collective-permute-start.2 = (bf16[18,1,256]{2,1,0:T(2,128)(2,1)S(1)}, bf16[18,1,256]{2,1,0:T(2,128)(2,1)S(1)}, u32[]{:S(2)}, u32[]{:S(2)}) collective-permute-start(bf16[18,1,256]{2,1,0:T(2,128)(2,1)S(1)} %get-tuple-element.169), channel_id=1, source_target_pairs={{0,1},{1,2},{2,3},{4,5},{5,6},{6,7},{8,9},{9,10},{10,11},{12,13},{... | collective-permute-start | bytes 27656 | tf_op jit(solution)/shard_map/ppermute | solution.py:17
  21.9 5.7 %collective-permute-start.3 = (bf16[18,1,256]{2,1,0:T(2,128)(2,1)S(1)}, bf16[18,1,256]{2,1,0:T(2,128)(2,1)S(1)}, u32[]{:S(2)}, u32[]{:S(2)}) collective-permute-start(bf16[18,1,256]{2,1,0:T(2,128)(2,1)S(1)} %get-tuple-element.170), channel_id=1, source_target_pairs={{1,0},{2,1},{3,2},{5,4},{6,5},{7,6},{9,8},{10,9},{11,10},{13,12},{... | collective-permute-start | bytes 27656 | tf_op jit(solution)/shard_map/ppermute | solution.py:18
  50.0 5.2 %copy-start.19 = (s32[8,1]{0,1:T(1,128)S(1)}, s32[8,1]{0,1:T(1,128)}, u32[]{:S(2)}) copy-start(s32[8,1]{0,1:T(1,128)} %param.16) | copy-start | bytes 100
  51.2 5.2 %copy-start.20 = (pred[8,5]{0,1:T(8,128)(4,1)S(1)}, pred[8,5]{0,1:T(8,128)(4,1)}, u32[]{:S(2)}) copy-start(pred[8,5]{0,1:T(8,128)(4,1)} %constant.129) | copy-start | bytes 124
  51.2 29.9 %all-to-all-start.1 = ((bf16[4,2,16,16,256]{4,3,2,1,0:T(8,128)(2,1)}), bf16[4,2,16,16,256]{4,3,2,1,0:T(8,128)(2,1)S(1)}, u32[]{:S(2)}, u32[]{:S(2)}) async-start(bf16[4,2,16,16,256]{4,3,2,1,0:T(8,128)(2,1)} %bitcast.140), calls=%async_computation.1 | async-start | bytes 2097152 | tf_op jit(solution)/shard_map/all_to_all | solution.py:109
  81.0 8.7 %all-to-all-start = ((bf16[4,2,4]{2,1,0:T(2,128)(2,1)}), bf16[4,2,4]{2,1,0:T(2,128)(2,1)S(1)}, u32[]{:S(2)}, u32[]{:S(2)}) async-start(bf16[4,2,4]{2,1,0:T(2,128)(2,1)} %bitcast.9), calls=%async_computation | async-start | bytes 4096 | tf_op jit(solution)/shard_map/all_to_all | solution.py:110
  90.2 0.7 copy-start.14
  92.2 1.3 copy-start.18
  94.7 1.2 copy-start.8
  94.7 1.8 copy-start.17
  100.3 0.8 copy-start.6
  105.3 6.1 %copy-start.4 = (bf16[14,4,16,256]{3,2,1,0:T(8,128)(2,1)}, bf16[14,4,16,256]{3,2,1,0:T(8,128)(2,1)S(1)}, u32[]{:S(2)}) copy-start(bf16[14,4,16,256]{3,2,1,0:T(8,128)(2,1)S(1)} %reshape.159) | copy-start | bytes 1376260
  116.3 5.3 %copy-start.10 = (bf16[4,14,14,256]{3,2,1,0:T(8,128)(2,1)S(1)}, bf16[4,14,14,256]{3,2,1,0:T(8,128)(2,1)}, u32[]{:S(2)}) copy-start(bf16[4,14,14,256]{3,2,1,0:T(8,128)(2,1)} %copy_bitcast_fusion.2) | copy-start | bytes 1204228
  118.1 22.3 %all-to-all-start.2 = ((bf16[4,2,14,14,256]{4,1,3,2,0:T(2,128)(2,1)}), bf16[4,2,14,14,256]{4,1,3,2,0:T(2,128)(2,1)S(1)}, u32[]{:S(2)}, u32[]{:S(2)}) async-start(bf16[4,2,14,14,256]{4,1,3,2,0:T(2,128)(2,1)} %copy.105), calls=%async_computation.2 | async-start | bytes 1605632 | tf_op jit(solution)/shard_map/all_to_all | solution.py:131
  121.6 1.5 copy-start.12
  121.6 163.3 %all-reduce.5.cloned.1.call-start = ((), (), s32[]{:S(2)}) async-start(), calls=%async_computation.3 | async-start | bytes 9437184 | tf_op jit(solution)/shard_map/psum | solution.py:136
  123.4 1.0 copy-start.13
  124.5 1.0 copy-start.5
  126.2 1.0 copy-start.11
  127.2 1.0 copy-start.7
  127.2 1.2 copy-start.9
  134.0 1.5 copy-start.2
  140.6 1.3 copy-start.15
  140.6 1.3 copy-start.16
  141.9 45.5 %copy-start.3 = (f32[16,8,5,256]{3,0,2,1:T(8,128)S(1)}, f32[16,8,5,256]{3,0,2,1:T(8,128)}, u32[]{:S(2)}) copy-start(f32[16,8,5,256]{3,0,2,1:T(8,128)} %copy.111) | copy-start | bytes 1966084
  187.6 2.6 collective-permute-start.4
  188.9 5.6 %collective-permute-start.5 = (bf16[1,32,256]{2,0,1:T(2,128)(2,1)S(1)}, bf16[1,32,256]{2,0,1:T(2,128)(2,1)S(1)}, u32[]{:S(2)}, u32[]{:S(2)}) collective-permute-start(bf16[1,32,256]{2,0,1:T(2,128)(2,1)S(1)} %get-tuple-element.172), channel_id=1, source_target_pairs={{4,0},{8,4},{12,8},{16,12},{20,16},{24,20},{28,24},{5,1},{9,5},{13... | collective-permute-start | bytes 49160 | tf_op jit(solution)/shard_map/ppermute | solution.py:18
  194.6 3.2 %collective-permute-start.6 = (bf16[18,1,256]{2,0,1:T(8,128)(2,1)S(1)}, bf16[18,1,256]{2,0,1:T(8,128)(2,1)S(1)}, u32[]{:S(2)}, u32[]{:S(2)}) collective-permute-start(bf16[18,1,256]{2,0,1:T(8,128)(2,1)S(1)} %get-tuple-element.167), channel_id=1, source_target_pairs={{0,1},{1,2},{2,3},{4,5},{5,6},{6,7},{8,9},{9,10},{10,11},{12,13},{... | collective-permute-start | bytes 27656 | tf_op jit(solution)/shard_map/ppermute | solution.py:17
  196.4 5.6 %collective-permute-start.7 = (bf16[18,1,256]{2,0,1:T(8,128)(2,1)S(1)}, bf16[18,1,256]{2,0,1:T(8,128)(2,1)S(1)}, u32[]{:S(2)}, u32[]{:S(2)}) collective-permute-start(bf16[18,1,256]{2,0,1:T(8,128)(2,1)S(1)} %get-tuple-element.168), channel_id=1, source_target_pairs={{1,0},{2,1},{3,2},{5,4},{6,5},{7,6},{9,8},{10,9},{11,10},{13,12},{... | collective-permute-start | bytes 27656 | tf_op jit(solution)/shard_map/ppermute | solution.py:18
  284.9 3.4 %copy-start.1 = (f32[3,3,256,256]{3,2,1,0:T(8,128)S(1)}, f32[3,3,256,256]{3,2,1,0:T(8,128)}, u32[]{:S(2)}) copy-start(f32[3,3,256,256]{3,2,1,0:T(8,128)} %get-tuple-element.154) | copy-start | bytes 7077892
Sparse Core Ops, SparseCore 0:
  138.8 146.0 all-reduce.4
where the time goes:
time: 298 us; the launch traced here: 297 us
  waiting for transfers between devices  123 us (41%)
  local copies, waits for them, and re-layouts  60.4 us (20%)
  loops' own time  31.5 us (11%)
  starting transfers between devices  27.2 us (9%)
  matrix products  27.2 us (9%)
  between operations  14.9 us (5%)
  other arithmetic  12.8 us (4%)
    psum x1, waiting for transfers between devices, body(): lax.psum((first_local, second_local), ('row', 'col'))  80.6 us
    another operation x1, loops' own time, body(): lax.fori_loop(0, slot_count, add_box, jnp.zeros((tile_rows, tile_cols, ch...  31.5 us
    all_to_all x1, waiting for transfers between devices, body(): lax.all_to_all(outgoing, 'col', split_axis=0, concat_axis=0, tiled=True)  22.7 us
    gather x24, local copies, waits for them, and re-layouts  19.9 us
    dot_general x18, matrix products, weight_grad(): lax.dot_general(window, flat_delta, (((0,), (0,)), ((), ())), preferred_e...  14 us
    ppermute x4, waiting for transfers between devices, padded_2(): after = lax.ppermute(leading, axis, down)  12.8 us
    ppermute x4, starting transfers between devices, padded_2(): before = lax.ppermute(last, axis, up)  11.1 us
    conv_general_dilated x7, matrix products, conv_pad(): lax.conv_general_dilated(inputs, kernel, (1, 1), ((margin, margin), (marg...  11.1 us
  transfers between devices with their start and end apart: 12, of which 9 were waited for; matrix products, arithmetic and copies ran while one was open for 13% of the time, Pallas kernels for 0%

commit v1 on v0

--- a/solution.py
+++ b/solution.py
@@ -5,6 +5,29 @@
 from jax.sharding import PartitionSpec as P
 
 LAYOUT = ("NHWC", "HWIO", "NHWC")
+
+
+def in_blocks(shard, dim, devices):
+    shape = shard.shape
+    tiles = shard.reshape(*shape[:dim], devices, shape[dim] // devices, *shape[dim + 1 :])
+    return jnp.moveaxis(tiles, dim, 0)
+
+
+def joined_along(blocks, dim):
+    shape = list(blocks.shape[1:])
+    shape[dim] *= blocks.shape[0]
+    return jnp.moveaxis(blocks, 0, dim).reshape(shape)
+
+
+def rotated_exchange(x, axis, split_dim, concat_dim):
+    length, index = (lax.axis_size(axis), lax.axis_index(axis))
+    blocks = in_blocks(x, split_dim, length)
+    outs = [blocks[index]]
+    for hop in range(1, length):
+        sent = blocks[(index + hop) % length]
+        outs.append(lax.ppermute(sent, axis, [(i, (i + hop) % length) for i in range(length)]))
+    blocks = jnp.stack(outs)[(index - jnp.arange(length)) % length]
+    return joined_along(blocks, concat_dim)
 
 
 def padded_2(shard, sides, width):
@@ -106,7 +129,7 @@
     )(top_row, left_col)
     outgoing = pick_rows(send_map, windows).reshape(columns, capacity, window, window, channels)
     arrived, arrived_head = (
-        lax.all_to_all(outgoing, "col", split_axis=0, concat_axis=0, tiled=True),
+        rotated_exchange(outgoing, "col", 0, 0),
         lax.all_to_all(pair_head, "col", split_axis=0, concat_axis=0, tiled=True),
     )
     arrived_head = arrived_head.reshape(pair_count, head_count)

time: 298 us -> 288 us (0.966)
  waiting for transfers between devices: 123 us -> 115 us
  local copies, waits for them, and re-layouts: 60.4 us -> 54.4 us
    all_to_all x1 -> x0, waiting for transfers between devices: 22.7 us -> none  [body(): lax.all_to_all(outgoing, 'col', split_axis=0, concat_axis=0, tiled=True)]
    ppermute x0 -> x3, waiting for transfers between devices: none -> 19.6 us  [rotated_exchange(): lax.ppermute(sent, axis, [(i, (i + hop) % length) for i in range(length)])]
    all_to_all x1, waiting for transfers between devices: 4.8 us -> 0.01 us  [body(): lax.all_to_all(pair_head, 'col', split_axis=0, concat_axis=0, tiled=True)]
    ppermute x0 -> x3, starting transfers between devices: none -> 4.44 us  [rotated_exchange(): lax.ppermute(sent, axis, [(i, (i + hop) % length) for i in range(length)])]
    all_to_all x1 -> x0, starting transfers between devices: 3.99 us -> none  [body(): lax.all_to_all(outgoing, 'col', split_axis=0, concat_axis=0, tiled=True)]
    gather x24 -> x25, local copies, waits for them, and re-layouts: 19.9 us -> 16.2 us
    unnamed x49 -> x47, local copies, waits for them, and re-layouts: 9.91 us -> 7.71 us
  transfers between devices with their start and end apart: 12 -> 14, of which waited for: 9 -> 9; matrix products, arithmetic and copies ran while one was open for 13% -> 19% of each run, Pallas kernels for 0% -> 0%
where the time goes in v1:
time: 288 us; the launch traced here: 286 us
  waiting for transfers between devices  115 us (40%)
  local copies, waits for them, and re-layouts  54.4 us (19%)
  loops' own time  31.7 us (11%)
  starting transfers between devices  29 us (10%)
  matrix products  27.2 us (9%)
  between operations  14.9 us (5%)
  other arithmetic  13.7 us (5%)
    psum x1, waiting for transfers between devices, body(): lax.psum((first_local, second_local), ('row', 'col'))  79.8 us
    another operation x1, loops' own time, body(): lax.fori_loop(0, slot_count, add_box, jnp.zeros((tile_rows, tile_cols, ch...  31.5 us
    ppermute x3, waiting for transfers between devices, rotated_exchange(): lax.ppermute(sent, axis, [(i, (i + hop) % length) for i in range(length)])  19.6 us
    gather x24, local copies, waits for them, and re-layouts  15.6 us
    dot_general x18, matrix products, weight_grad(): lax.dot_general(window, flat_delta, (((0,), (0,)), ((), ())), preferred_e...  14 us
    ppermute x4, waiting for transfers between devices, padded_2(): after = lax.ppermute(leading, axis, down)  12.4 us
    conv_general_dilated x7, matrix products, conv_pad(): lax.conv_general_dilated(inputs, kernel, (1, 1), ((margin, margin), (marg...  11.3 us
    ppermute x4, starting transfers between devices, padded_2(): before = lax.ppermute(last, axis, up)  9.54 us
  transfers between devices with their start and end apart: 14, of which 9 were waited for; matrix products, arithmetic and copies ran while one was open for 19% of the time, Pallas kernels for 0%

profile of v1, /device:TPU:0, one launch (start us, length us, event | category | flops | bytes accessed | tf_op | source)
XLA Modules:
  0.0 286.0 jit_solution(11104835893836966281)
XLA Ops:
  11.7 6.3 %all-to-all-start = ((bf16[4,2,4]{2,1,0:T(2,128)(2,1)}), bf16[4,2,4]{2,1,0:T(2,128)(2,1)S(1)}, u32[]{:S(2)}, u32[]{:S(2)}) async-start(bf16[4,2,4]{2,1,0:T(2,128)(2,1)} %bitcast.9), calls=%async_computation | async-start | bytes 4096 | tf_op jit(solution)/shard_map/all_to_all | solution.py:133
  18.8 1.3 collective-permute-start.1
  20.1 3.0 %collective-permute-start = (bf16[1,32,256]{2,1,0:T(8,128)(2,1)S(1)}, bf16[1,32,256]{2,1,0:T(8,128)(2,1)S(1)}, u32[]{:S(2)}, u32[]{:S(2)}) collective-permute-start(bf16[1,32,256]{2,1,0:T(8,128)(2,1)S(1)} %get-tuple-element.178), channel_id=1, source_target_pairs={{0,4},{4,8},{8,12},{12,16},{16,20},{20,24},{24,28},{1,5},{5,9},{9,... | collective-permute-start | bytes 49160 | tf_op jit(solution)/shard_map/ppermute | solution.py:40
  25.0 3.9 %collective-permute-start.2 = (bf16[18,1,256]{2,1,0:T(2,128)(2,1)S(1)}, bf16[18,1,256]{2,1,0:T(2,128)(2,1)S(1)}, u32[]{:S(2)}, u32[]{:S(2)}) collective-permute-start(bf16[18,1,256]{2,1,0:T(2,128)(2,1)S(1)} %get-tuple-element.173), channel_id=1, source_target_pairs={{0,1},{1,2},{2,3},{4,5},{5,6},{6,7},{8,9},{9,10},{10,11},{12,13},{... | collective-permute-start | bytes 27656 | tf_op jit(solution)/shard_map/ppermute | solution.py:40
  28.9 1.3 collective-permute-start.3
  30.4 4.3 %collective-permute-done.3 = bf16[18,1,256]{2,1,0:T(2,128)(2,1)S(1)} collective-permute-done((bf16[18,1,256]{2,1,0:T(2,128)(2,1)S(1)}, bf16[18,1,256]{2,1,0:T(2,128)(2,1)S(1)}, u32[]{:S(2)}, u32[]{:S(2)}) %collective-permute-start.3) | collective-permute-done | bytes 9248 | tf_op jit(solution)/shard_map/ppermute | solution.py:41
  35.1 15.8 %while.15 = (s32[]{:T(128)}, bf16[18,34,256]{2,1,0:T(8,128)(2,1)S(1)}, s32[8,3]{0,1:T(4,128)S(1)}, bf16[8,16,16,256]{3,2,1,0:T(8,128)(2,1)S(1)}, s32[]{:T(128)}) while((s32[]{:T(128)}, bf16[18,34,256]{2,1,0:T(8,128)(2,1)S(1)}, s32[8,3]{0,1:T(4,128)S(1)}, bf16[8,16,16,256]{3,2,1,0:T(8,128)(2,1)S(1)}, s32[]{:T(128)}) %tuple.67), condition=%wide.while_cond, body=%wide.while_body.sunk | while | flops 2 | bytes 262269 | solution.py:128
  35.7 1.3 bitcast_dynamic-update-slice_fusion.2
  37.7 1.3 bitcast_dynamic-update-slice_fusion.2
  39.7 1.3 bitcast_dynamic-update-slice_fusion.2
  41.6 1.3 bitcast_dynamic-update-slice_fusion.2
  43.6 1.3 bitcast_dynamic-update-slice_fusion.2
  45.6 1.3 bitcast_dynamic-update-slice_fusion.2
  47.6 1.3 bitcast_dynamic-update-slice_fusion.2
  49.5 1.3 bitcast_dynamic-update-slice_fusion.2
  52.2 1.5 collective-permute-start.6
  53.7 1.5 collective-permute-start.5
  55.2 1.5 collective-permute-start.4
  57.6 1.1 copy.111
  58.7 1.9 collective-permute-done.6
  60.5 17.7 %collective-permute-done.5 = bf16[1,2,16,16,256]{4,3,2,1,0:T(8,128)(2,1)S(1)} collective-permute-done((bf16[1,2,16,16,256]{4,3,2,1,0:T(8,128)(2,1)S(1)}, bf16[1,2,16,16,256]{4,3,2,1,0:T(8,128)(2,1)S(1)}, u32[]{:S(2)}, u32[]{:S(2)}) %collective-permute-start.5) | collective-permute-done | bytes 262176 | tf_op jit(solution)/shard_map/ppermute | solution.py:28
  80.6 1.3 multiply_convert_fusion.1
  83.2 1.2 fusion.43
  84.4 1.1 select_bitcast_fusion.1
  86.2 1.3 add_multiply_fusion
  88.8 1.2 fusion.62
  91.4 2.9 %fusion.9 = bf16[14,32,2,256]{3,1,2,0:T(8,128)(2,1)S(1)} fusion(bf16[3,3,256,256]{3,2,1,0:T(8,128)(2,1)} %param.13, bf16[14,4,7,2,256]{4,2,1,3,0:T(8,128)(2,1)S(1)} %slice.140, bf16[14,4,8,2,256]{4,2,1,3,0:T(8,128)(2,1)S(1)} %copy.102, f32[14,32,2,256]{3,1,2,0:T(8,128)} %copy-done.8, pred[32,2]{0,1:T(4,128)(4,1)S(1)} %copy-done.14), kind=kOutput, calls=%fused_computation.24 | convolution fusion | flops 1011679232 | bytes 3416128 | tf_op jit(solution)/shard_map/conv_general_dilated | solution.py:47
  95.9 2.3 copy.120
  98.2 1.2 reshape.205
  101.2 2.8 convolution_convert_fusion.4
  106.1 1.8 copy.105
  107.8 3.5 %all-to-all-start.1 = ((bf16[4,2,14,14,256]{4,1,3,2,0:T(2,128)(2,1)}), bf16[4,2,14,14,256]{4,1,3,2,0:T(2,128)(2,1)S(1)}, u32[]{:S(2)}, u32[]{:S(2)}) async-start(bf16[4,2,14,14,256]{4,1,3,2,0:T(2,128)(2,1)} %copy.105), calls=%async_computation.1 | async-start | bytes 1605632 | tf_op jit(solution)/shard_map/all_to_all | solution.py:154
  111.4 1.4 fusion.28
  120.2 1.1 fusion.17
  123.7 1.3 fusion.14
  125.2 1.1 fusion.13
  127.3 1.1 fusion.11
  128.4 3.0 %all-to-all-done.1 = bf16[4,2,14,14,256]{4,1,3,2,0:T(2,128)(2,1)S(1)} async-done(((bf16[4,2,14,14,256]{4,1,3,2,0:T(2,128)(2,1)}), bf16[4,2,14,14,256]{4,1,3,2,0:T(2,128)(2,1)S(1)}, u32[]{:S(2)}, u32[]{:S(2)}) %all-to-all-start.1) | async-done | bytes 802848 | tf_op jit(solution)/shard_map/all_to_all | solution.py:154
  132.8 45.5 %while.14 = (s32[]{:T(128)}, f32[16,32,256]{2,0,1:T(8,128)S(1)}, s32[8]{0:T(128)S(1)}, s32[8]{0:T(128)S(1)}, bf16[8,14,14,256]{3,2,1,0:T(8,128)(2,1)S(1)}, /*index=5*/s32[]{:T(128)}, s32[]{:T(128)}, s32[]{:T(128)}, s32[]{:T(128)}) while((s32[]{:T(128)}, f32[16,32,256]{2,0,1:T(8,128)S(1)}, s32[8]{0:T(128)S(1)}, s32[8]{0:T(128)S(1)}, ...), condition=%wide.region_2.3_spmd, body=%wide.region_1.2_spmd.sunk | while | flops 100360 | bytes 1706193 | solution.py:171
  178.6 1.3 collective-permute-start.7
  179.9 1.3 collective-permute-start.8
  181.2 3.7 %collective-permute-done.8 = bf16[1,32,256]{2,0,1:T(2,128)(2,1)S(1)} collective-permute-done((bf16[1,32,256]{2,0,1:T(2,128)(2,1)S(1)}, bf16[1,32,256]{2,0,1:T(2,128)(2,1)S(1)}, u32[]{:S(2)}, u32[]{:S(2)}) %collective-permute-start.8) | collective-permute-done | bytes 16416 | tf_op jit(solution)/shard_map/ppermute | solution.py:41
  184.9 1.3 collective-permute-start.9
  186.2 1.3 collective-permute-start.10
  187.6 4.4 %collective-permute-done.10 = bf16[18,1,256]{2,0,1:T(8,128)(2,1)S(1)} collective-permute-done((bf16[18,1,256]{2,0,1:T(8,128)(2,1)S(1)}, bf16[18,1,256]{2,0,1:T(8,128)(2,1)S(1)}, u32[]{:S(2)}, u32[]{:S(2)}) %collective-permute-start.10) | collective-permute-done | bytes 9248 | tf_op jit(solution)/shard_map/ppermute | solution.py:41
  194.3 79.8 %all-reduce.5.cloned.1.call-done = (f32[3,3,256,256]{3,2,1,0:T(8,128)}, f32[3,3,256,256]{3,2,1,0:T(8,128)}) async-done(((f32[3,3,256,256]{3,2,1,0:T(8,128)}, f32[3,3,256,256]{3,2,1,0:T(8,128)}), (f32[3,3,256,256]{3,2,1,0:T(8,128)}, f32[3,3,256,256]{3,2,1,0:T(8,128)})) %all-reduce.5.cloned.1.call-update) | async-done | bytes 4718608 | tf_op jit(solution)/shard_map/psum | solution.py:159
  274.1 3.4 %broadcast_multiply_fusion.1 = f32[3,3,256,256]{3,2,1,0:T(8,128)} fusion(f32[3,3,256,256]{3,2,1,0:T(8,128)} %get-tuple-element.153), kind=kLoop, calls=%fused_computation.30 | loop fusion | flops 589824 | bytes 4718592 | tf_op jit(solution)/shard_map/mul | solution.py:177
  277.5 1.6 broadcast_multiply_fusion
  (203 shorter events, 56.1 us)
Async XLA Ops:
  7.2 49.5 %copy-start = (bf16[3,3,256,256]{3,2,1,0:T(8,128)(2,1)S(1)}, bf16[3,3,256,256]{3,2,1,0:T(8,128)(2,1)}, u32[]{:S(2)}) copy-start(bf16[3,3,256,256]{3,2,1,0:T(8,128)(2,1)} %param.11) | copy-start | bytes 3538948
  11.7 67.8 %all-to-all-start = ((bf16[4,2,4]{2,1,0:T(2,128)(2,1)}), bf16[4,2,4]{2,1,0:T(2,128)(2,1)S(1)}, u32[]{:S(2)}, u32[]{:S(2)}) async-start(bf16[4,2,4]{2,1,0:T(2,128)(2,1)} %bitcast.9), calls=%async_computation | async-start | bytes 4096 | tf_op jit(solution)/shard_map/all_to_all | solution.py:133
  18.8 6.1 %collective-permute-start.1 = (bf16[1,32,256]{2,1,0:T(8,128)(2,1)S(1)}, bf16[1,32,256]{2,1,0:T(8,128)(2,1)S(1)}, u32[]{:S(2)}, u32[]{:S(2)}) collective-permute-start(bf16[1,32,256]{2,1,0:T(8,128)(2,1)S(1)} %get-tuple-element.177), channel_id=1, source_target_pairs={{4,0},{8,4},{12,8},{16,12},{20,16},{24,20},{28,24},{5,1},{9,5},{13... | collective-permute-start | bytes 49160 | tf_op jit(solution)/shard_map/ppermute | solution.py:41
  20.1 3.9 %collective-permute-start = (bf16[1,32,256]{2,1,0:T(8,128)(2,1)S(1)}, bf16[1,32,256]{2,1,0:T(8,128)(2,1)S(1)}, u32[]{:S(2)}, u32[]{:S(2)}) collective-permute-start(bf16[1,32,256]{2,1,0:T(8,128)(2,1)S(1)} %get-tuple-element.178), channel_id=1, source_target_pairs={{0,4},{4,8},{8,12},{12,16},{16,20},{20,24},{24,28},{1,5},{5,9},{9,... | collective-permute-start | bytes 49160 | tf_op jit(solution)/shard_map/ppermute | solution.py:40
  25.0 5.4 %collective-permute-start.2 = (bf16[18,1,256]{2,1,0:T(2,128)(2,1)S(1)}, bf16[18,1,256]{2,1,0:T(2,128)(2,1)S(1)}, u32[]{:S(2)}, u32[]{:S(2)}) collective-permute-start(bf16[18,1,256]{2,1,0:T(2,128)(2,1)S(1)} %get-tuple-element.173), channel_id=1, source_target_pairs={{0,1},{1,2},{2,3},{4,5},{5,6},{6,7},{8,9},{9,10},{10,11},{12,13},{... | collective-permute-start | bytes 27656 | tf_op jit(solution)/shard_map/ppermute | solution.py:40
  28.9 5.7 %collective-permute-start.3 = (bf16[18,1,256]{2,1,0:T(2,128)(2,1)S(1)}, bf16[18,1,256]{2,1,0:T(2,128)(2,1)S(1)}, u32[]{:S(2)}, u32[]{:S(2)}) collective-permute-start(bf16[18,1,256]{2,1,0:T(2,128)(2,1)S(1)} %get-tuple-element.174), channel_id=1, source_target_pairs={{1,0},{2,1},{3,2},{5,4},{6,5},{7,6},{9,8},{10,9},{11,10},{13,12},{... | collective-permute-start | bytes 27656 | tf_op jit(solution)/shard_map/ppermute | solution.py:41
  51.9 4.8 %copy-start.19 = (pred[8,5]{0,1:T(8,128)(4,1)S(1)}, pred[8,5]{0,1:T(8,128)(4,1)}, u32[]{:S(2)}) copy-start(pred[8,5]{0,1:T(8,128)(4,1)} %constant.160) | copy-start | bytes 124
  52.2 8.3 %collective-permute-start.6 = (bf16[1,2,16,16,256]{4,3,2,1,0:T(8,128)(2,1)S(1)}, bf16[1,2,16,16,256]{4,3,2,1,0:T(8,128)(2,1)S(1)}, u32[]{:S(2)}, u32[]{:S(2)}) collective-permute-start(bf16[1,2,16,16,256]{4,3,2,1,0:T(8,128)(2,1)S(1)} %get-tuple-element.160), channel_id=1, source_target_pairs={{0,3},{1,0},{2,1},{3,2},{4,7},{5,4},{6,5},{7,6},{8,11},{9,8},{10,9... | collective-permute-start | bytes 786440 | tf_op jit(solution)/shard_map/ppermute | solution.py:28
  53.7 24.5 %collective-permute-start.5 = (bf16[1,2,16,16,256]{4,3,2,1,0:T(8,128)(2,1)S(1)}, bf16[1,2,16,16,256]{4,3,2,1,0:T(8,128)(2,1)S(1)}, u32[]{:S(2)}, u32[]{:S(2)}) collective-permute-start(bf16[1,2,16,16,256]{4,3,2,1,0:T(8,128)(2,1)S(1)} %get-tuple-element.161), channel_id=1, source_target_pairs={{0,2},{1,3},{2,0},{3,1},{4,6},{5,7},{6,4},{7,5},{8,10},{9,11},{10,... | collective-permute-start | bytes 786440 | tf_op jit(solution)/shard_map/ppermute | solution.py:28
  55.2 23.0 %collective-permute-start.4 = (bf16[1,2,16,16,256]{4,3,2,1,0:T(8,128)(2,1)S(1)}, bf16[1,2,16,16,256]{4,3,2,1,0:T(8,128)(2,1)S(1)}, u32[]{:S(2)}, u32[]{:S(2)}) collective-permute-start(bf16[1,2,16,16,256]{4,3,2,1,0:T(8,128)(2,1)S(1)} %get-tuple-element.162), channel_id=1, source_target_pairs={{0,1},{1,2},{2,3},{3,0},{4,5},{5,6},{6,7},{7,4},{8,9},{9,10},{10,1... | collective-permute-start | bytes 786440 | tf_op jit(solution)/shard_map/ppermute | solution.py:28
  80.0 0.7 copy-start.14
  81.9 1.3 copy-start.18
  84.4 1.2 copy-start.8
  84.4 1.8 copy-start.17
  90.0 0.8 copy-start.6
  95.0 6.2 %copy-start.4 = (bf16[14,4,16,256]{3,2,1,0:T(8,128)(2,1)}, bf16[14,4,16,256]{3,2,1,0:T(8,128)(2,1)S(1)}, u32[]{:S(2)}) copy-start(bf16[14,4,16,256]{3,2,1,0:T(8,128)(2,1)S(1)} %reshape.200) | copy-start | bytes 1376260
  106.1 5.3 %copy-start.10 = (bf16[4,14,14,256]{3,2,1,0:T(8,128)(2,1)S(1)}, bf16[4,14,14,256]{3,2,1,0:T(8,128)(2,1)}, u32[]{:S(2)}) copy-start(bf16[4,14,14,256]{3,2,1,0:T(8,128)(2,1)} %copy_bitcast_fusion.2) | copy-start | bytes 1204228
  107.8 23.5 %all-to-all-start.1 = ((bf16[4,2,14,14,256]{4,1,3,2,0:T(2,128)(2,1)}), bf16[4,2,14,14,256]{4,1,3,2,0:T(2,128)(2,1)S(1)}, u32[]{:S(2)}, u32[]{:S(2)}) async-start(bf16[4,2,14,14,256]{4,1,3,2,0:T(2,128)(2,1)} %copy.105), calls=%async_computation.1 | async-start | bytes 1605632 | tf_op jit(solution)/shard_map/all_to_all | solution.py:154
  111.3 1.5 copy-start.12
  111.3 162.8 %all-reduce.5.cloned.1.call-start = ((), (), s32[]{:S(2)}) async-start(), calls=%async_computation.2 | async-start | bytes 9437184 | tf_op jit(solution)/shard_map/psum | solution.py:159
  113.2 1.0 copy-start.13
  114.2 1.0 copy-start.5
  115.9 1.0 copy-start.11
  117.0 1.0 copy-start.7
  117.0 1.2 copy-start.9
  123.7 1.5 copy-start.2
  131.5 1.3 copy-start.15
  131.5 1.3 copy-start.16
  132.8 45.5 %copy-start.3 = (f32[16,8,5,256]{3,0,2,1:T(8,128)S(1)}, f32[16,8,5,256]{3,0,2,1:T(8,128)}, u32[]{:S(2)}) copy-start(f32[16,8,5,256]{3,0,2,1:T(8,128)} %copy.111) | copy-start | bytes 1966084
  178.6 2.6 collective-permute-start.7
  179.9 5.0 %collective-permute-start.8 = (bf16[1,32,256]{2,0,1:T(2,128)(2,1)S(1)}, bf16[1,32,256]{2,0,1:T(2,128)(2,1)S(1)}, u32[]{:S(2)}, u32[]{:S(2)}) collective-permute-start(bf16[1,32,256]{2,0,1:T(2,128)(2,1)S(1)} %get-tuple-element.176), channel_id=1, source_target_pairs={{4,0},{8,4},{12,8},{16,12},{20,16},{24,20},{28,24},{5,1},{9,5},{13... | collective-permute-start | bytes 49160 | tf_op jit(solution)/shard_map/ppermute | solution.py:41
  184.9 2.7 collective-permute-start.9
  186.2 5.8 %collective-permute-start.10 = (bf16[18,1,256]{2,0,1:T(8,128)(2,1)S(1)}, bf16[18,1,256]{2,0,1:T(8,128)(2,1)S(1)}, u32[]{:S(2)}, u32[]{:S(2)}) collective-permute-start(bf16[18,1,256]{2,0,1:T(8,128)(2,1)S(1)} %get-tuple-element.172), channel_id=1, source_target_pairs={{1,0},{2,1},{3,2},{5,4},{6,5},{7,6},{9,8},{10,9},{11,10},{13,12},{... | collective-permute-start | bytes 27656 | tf_op jit(solution)/shard_map/ppermute | solution.py:41
  274.1 3.4 %copy-start.1 = (f32[3,3,256,256]{3,2,1,0:T(8,128)S(1)}, f32[3,3,256,256]{3,2,1,0:T(8,128)}, u32[]{:S(2)}) copy-start(f32[3,3,256,256]{3,2,1,0:T(8,128)} %get-tuple-element.154) | copy-start | bytes 7077892
Sparse Core Ops, SparseCore 0:
  128.5 145.5 all-reduce.4
